TPU v7x, 256 devices: a whole 4x4x8 slice. The times are simulated.
256 devices in a mesh: depth: 32 (over z, x_hi, core), shot: 8 (over y, x_lo).
Axes of the slice: x: 4 (x_hi: 2, x_lo: 2; x = x_hi * 2 + x_lo), y: 4, z: 8, core: 2. Of those that a mesh axis runs over, the one named last changes fastest.
Arguments:
- courant: float32 [512, 64, 128], P('depth'), may hold values from 0.04 to 0.2
- wave_before: float32 [8, 512, 64, 128], P('shot', 'depth'), may hold values from -10 to 10
- wave_current: float32 [8, 512, 64, 128], P('shot', 'depth'), may hold values from -10 to 10
- adjoint_after: float32 [8, 512, 64, 128], P('shot', 'depth'), may hold values from -10 to 10
- adjoint_current: float32 [8, 512, 64, 128], P('shot', 'depth'), may hold values from -10 to 10
- source_cell: int32 [8], P('shot'), may hold values from 0 to 4194303
- wavelet: float32 [8, 4], P('shot'), may hold values from -15 to 15
- receiver_cell: int32 [8, 256], P('shot'), may hold values from 0 to 4194303
- residual: float32 [8, 4, 256], P('shot'), may hold values from -12 to 12
- history: float32 [2, 5, 512, 64, 128], P(None, None, 'depth', 'shot'), may hold values from -23 to 23, as said below
Outputs:
- gradient: float32 [512, 64, 128], P('depth', 'shot')
- direction: float32 [512, 64, 128], P('depth', 'shot')
- courant_next: float32 [512, 64, 128], P('depth')
Inputs may be any that keep to these rules, and one draw needn't show every extreme that they name: In every pair the sum over all cells of history[0] times history[1] is positive.
All inputs are finite; a program needn't handle non-finite values.
Results may differ from a plain program's by a relative error of at most 0.00026.
Values sent between devices are 32-bit elements; how exact they have to be, the bound alone decides.
A program may use at most 128 MiB of HBM per device.

v0:
```python
import jax
import jax.numpy as jnp
from jax import lax
from jax.sharding import PartitionSpec as P

STEPS = 4
PAIRS = 5
coefficients = (-205.0 / 72.0, 8.0 / 5.0, -1.0 / 5.0, 8.0 / 315.0, -1.0 / 560.0)


def with_halo(cells, sides, width):
    for axis, dim in sides:
        count = lax.axis_size(axis)
        ends = count - 1
        head = lax.slice_in_dim(cells, 0, width, axis=dim)
        tail = lax.slice_in_dim(cells, cells.shape[dim] - width, cells.shape[dim], axis=dim)
        cells = jnp.concatenate(
            [
                lax.ppermute(tail, axis, [(i, (i + 1) % count) for i in range(ends)]),
                cells,
                lax.ppermute(head, axis, [((i + 1) % count, i) for i in range(ends)]),
            ],
            axis=dim,
        )
    return cells


def laplace_core(extended):
    interior = extended[4:-4]
    count_rows = interior.shape[0]
    width_x = interior.shape[1]
    width_y = interior.shape[2]
    padded = jnp.pad(interior, ((0, 0), (4, 4), (4, 4)))
    summed = 3.0 * coefficients[0] * interior
    for reach in range(1, 5):
        weight = coefficients[reach]
        summed = summed + weight * (
            extended[4 + reach : 4 + reach + count_rows]
            + extended[4 - reach : 4 - reach + count_rows]
        )
        summed = summed + weight * (
            padded[:, 4 + reach : 4 + reach + width_x, 4 : 4 + width_y]
            + padded[:, 4 - reach : 4 - reach + width_x, 4 : 4 + width_y]
        )
        summed = summed + weight * (
            padded[:, 4 : 4 + width_x, 4 + reach : 4 + reach + width_y]
            + padded[:, 4 : 4 + width_x, 4 - reach : 4 - reach + width_y]
        )
    return summed


def inject(volume, cell_ids, values, offset):
    count_rows = volume.shape[0]
    plane_size = volume.shape[1] * volume.shape[2]
    depth_row = cell_ids // plane_size - offset
    remainder = cell_ids % plane_size
    inside = (depth_row >= 0) & (depth_row < count_rows)
    row_safe = jnp.clip(depth_row, 0, count_rows - 1)
    return volume.at[row_safe, remainder // volume.shape[2], remainder % volume.shape[2]].add(
        jnp.where(inside, values, jnp.zeros_like(values))
    )


def per_device(
    courant,
    wave_before,
    wave_current,
    adjoint_after,
    adjoint_current,
    source_cell,
    wavelet,
    receiver_cell,
    residual,
    history,
):
    slab_rows = courant.shape[0]
    first_row = lax.axis_index("depth") * slab_rows
    shot_count = lax.axis_size("shot")
    summed = jnp.zeros(courant.shape, jnp.float32)
    laplacians = []
    wave_old = wave_before[0]
    wave_now = wave_current[0]
    for moment in range(STEPS):
        extended = with_halo(wave_now, (("depth", 0),), 4)
        laplacian = laplace_core(extended)
        wave_new = 2.0 * wave_now - wave_old + courant * laplacian
        wave_new = inject(wave_new, source_cell, wavelet[0, moment : moment + 1], first_row)
        laplacians.append(laplacian)
        wave_old, wave_now = (wave_now, wave_new)
    adjoint_old = adjoint_after[0]
    adjoint_now = adjoint_current[0]
    for moment in reversed(range(STEPS)):
        extended = with_halo(courant * adjoint_now, (("depth", 0),), 4)
        adjoint_new = 2.0 * adjoint_now - adjoint_old + laplace_core(extended)
        adjoint_new = inject(adjoint_new, receiver_cell[0], residual[0, moment], first_row)
        summed = summed + adjoint_new * laplacians[moment]
        adjoint_old, adjoint_now = (adjoint_now, adjoint_new)
    grad_piece = lax.psum_scatter(summed, "shot", scatter_dimension=1, tiled=True) * (
        1.0 / (shot_count * STEPS)
    )
    displaced = history[0]
    changes = history[1]
    step_change = jnp.einsum("izxy,jzxy->ij", displaced, changes, precision=lax.Precision.HIGHEST)
    change_change = jnp.einsum("izxy,jzxy->ij", changes, changes, precision=lax.Precision.HIGHEST)
    step_grad = jnp.sum(displaced * grad_piece, axis=(1, 2, 3))
    change_grad = jnp.sum(changes * grad_piece, axis=(1, 2, 3))
    packed = jnp.concatenate(
        [step_change, change_change, step_grad[None], change_grad[None]], axis=0
    )
    packed = lax.psum(packed, ("depth", "shot"))
    step_change = packed[:PAIRS]
    change_change = packed[PAIRS : 2 * PAIRS]
    step_grad = packed[2 * PAIRS]
    change_grad = packed[2 * PAIRS + 1]
    inverse = [1.0 / step_change[i, i] for i in range(PAIRS)]
    alphas = [None] * PAIRS
    for i in reversed(range(PAIRS)):
        value = step_grad[i]
        for j in range(i + 1, PAIRS):
            value = value - alphas[j] * step_change[i, j]
        alphas[i] = inverse[i] * value
    gamma = step_change[PAIRS - 1, PAIRS - 1] / change_change[PAIRS - 1, PAIRS - 1]
    gains = []
    for i in range(PAIRS):
        value = change_grad[i]
        for j in range(PAIRS):
            value = value - alphas[j] * change_change[i, j]
        value = gamma * value
        for j in range(i):
            value = value + gains[j] * step_change[j, i]
        gains.append(alphas[i] - inverse[i] * value)
    scaled = grad_piece
    for i in range(PAIRS):
        scaled = scaled - alphas[i] * changes[i]
    scaled = gamma * scaled
    for i in range(PAIRS):
        scaled = scaled + gains[i] * displaced[i]
    direction = -scaled
    piece_width = grad_piece.shape[1]
    own_courant = lax.dynamic_slice_in_dim(
        courant, lax.axis_index("shot") * piece_width, piece_width, 1
    )
    next_piece = own_courant + 0.05 * direction
    courant_next = lax.all_gather(next_piece, "shot", axis=1, tiled=True)
    return (grad_piece, direction, courant_next)


def solution(mesh):
    return jax.shard_map(
        per_device,
        mesh=mesh,
        in_specs=(
            P("depth", None, None),
            P("shot", "depth", None, None),
            P("shot", "depth", None, None),
            P("shot", "depth", None, None),
            P("shot", "depth", None, None),
            P("shot"),
            P("shot", None),
            P("shot", None),
            P("shot", None, None),
            P(None, None, "depth", "shot", None),
        ),
        out_specs=(P("depth", "shot", None), P("depth", "shot", None), P("depth", None, None)),
        check_vma=False,
    )
```

profile of v0, /device:TPU:32, one launch (start us, length us, event | category | flops | bytes accessed | tf_op | source)
XLA Modules:
  0.0 397.9 jit_solution(11437620847095359479)
XLA Ops:
  7.2 1.3 bitcast_multiply_fusion
  8.6 4.0 %collective-permute-start = (f32[4,64,128]{2,1,0:T(8,128)S(1)}, f32[4,64,128]{2,1,0:T(8,128)S(1)}, u32[]{:S(2)}, u32[]{:S(2)}) collective-permute-start(f32[4,64,128]{2,1,0:T(8,128)S(1)} %get-tuple-element.70), channel_id=1, source_target_pairs={{8,0},{16,8},{24,16},{32,24},{40,32},{48,40},{56,48},{64,56},{72,6... | collective-permute-start | bytes 393224 | tf_op jit(solution)/shard_map/ppermute | solution.py:21
  12.7 1.9 collective-permute-start.1
  14.7 6.0 %collective-permute-start.2 = (f32[4,64,128]{2,1,0:T(8,128)S(1)}, f32[4,64,128]{2,1,0:T(8,128)S(1)}, u32[]{:S(2)}, u32[]{:S(2)}) collective-permute-start(f32[4,64,128]{2,1,0:T(8,128)S(1)} %get-tuple-element.68), channel_id=1, source_target_pairs={{8,0},{16,8},{24,16},{32,24},{40,32},{48,40},{56,48},{64,56},{72,6... | collective-permute-start | bytes 393224 | tf_op jit(solution)/shard_map/ppermute | solution.py:21
  20.7 1.9 collective-permute-start.3
  23.3 0.7 fusion.369
  26.7 0.7 and_reduce_fusion
  27.4 1.9 fusion.184
  29.4 23.9 %scatter_fusion = f32[16,64,128]{2,1,0:T(8,128)S(1)} fusion(f32[16,64,128]{2,1,0:T(8,128)S(1)} %fusion.184, s32[256]{0:T(256)S(1)} %bitcast.180, f32[256]{0:T(256)} %get-tuple-element.128), kind=kCustom, calls=%fused_computation | custom fusion | flops 256 | bytes 6144 | tf_op jit(solution)/shard_map/scatter-add | solution.py:59
  53.4 3.7 fusion.348
  57.0 0.7 dynamic-slice.24
  59.8 6.1 %collective-permute-start.10 = (f32[4,64,128]{2,1,0:T(8,128)S(1)}, f32[4,64,128]{2,1,0:T(8,128)S(1)}, u32[]{:S(2)}, u32[]{:S(2)}) collective-permute-start(f32[4,64,128]{2,1,0:T(8,128)S(1)} %get-tuple-element.59), channel_id=1, source_target_pairs={{8,0},{16,8},{24,16},{32,24},{40,32},{48,40},{56,48},{64,56},{72,6... | collective-permute-start | bytes 393224 | tf_op jit(solution)/shard_map/ppermute | solution.py:21
  65.9 1.9 collective-permute-start.11
  67.8 0.7 fusion.363
  68.5 6.0 %collective-permute-start.4 = (f32[4,64,128]{2,1,0:T(8,128)}, f32[4,64,128]{2,1,0:T(8,128)S(1)}, u32[]{:S(2)}, u32[]{:S(2)}) collective-permute-start(f32[4,64,128]{2,1,0:T(8,128)} %get-tuple-element.66), channel_id=1, source_target_pairs={{8,0},{16,8},{24,16},{32,24},{40,32},{48,40},{56,48},{64,56},{72,6... | collective-permute-start | bytes 393224 | tf_op jit(solution)/shard_map/ppermute | solution.py:21
  74.5 1.9 collective-permute-start.5
  76.5 9.1 %fusion.59 = f32[16,64,128]{2,1,0:T(8,128)S(1)} fusion(f32[16,64,128]{2,1,0:T(8,128)} %copy-done.6, f32[4,64,128]{2,1,0:T(8,128)S(1)} %collective-permute-done.11, f32[4,64,128]{2,1,0:T(8,128)S(1)} %collective-permute-done.10, f32[1,16,64,128]{3,2,1,0:T(8,128)S(1)} %copy-done.2, f32[16,64,128]{2,1,0:T(8,128)S(1)} %scatter_fusion), kind=kLoop, calls=%fused_computation.289 | loop fusion | flops 6291456 | bytes 2359296 | tf_op jit(solution)/shard_map/add | solution.py:94
  85.6 15.2 %scatter_fusion.1 = f32[16,64,128]{2,1,0:T(8,128)S(1)} fusion(f32[16,64,128]{2,1,0:T(8,128)S(1)} %fusion.59, s32[256]{0:T(256)S(1)} %bitcast.181, f32[256]{0:T(256)S(1)} %get-tuple-element.127), kind=kCustom, calls=%fused_computation.1 | custom fusion | flops 256 | bytes 6144 | tf_op jit(solution)/shard_map/scatter-add | solution.py:59
  100.9 2.7 multiply_add_fusion.1
  103.6 6.1 %collective-permute-start.12 = (f32[4,64,128]{2,1,0:T(8,128)S(1)}, f32[4,64,128]{2,1,0:T(8,128)S(1)}, u32[]{:S(2)}, u32[]{:S(2)}) collective-permute-start(f32[4,64,128]{2,1,0:T(8,128)S(1)} %get-tuple-element.56), channel_id=1, source_target_pairs={{8,0},{16,8},{24,16},{32,24},{40,32},{48,40},{56,48},{64,56},{72,6... | collective-permute-start | bytes 393224 | tf_op jit(solution)/shard_map/ppermute | solution.py:21
  109.7 1.9 collective-permute-start.13
  111.6 0.6 dynamic-slice.25
  114.3 0.7 fusion.362
  115.0 6.0 %collective-permute-start.6 = (f32[4,64,128]{2,1,0:T(8,128)}, f32[4,64,128]{2,1,0:T(8,128)S(1)}, u32[]{:S(2)}, u32[]{:S(2)}) collective-permute-start(f32[4,64,128]{2,1,0:T(8,128)} %get-tuple-element.64), channel_id=1, source_target_pairs={{8,0},{16,8},{24,16},{32,24},{40,32},{48,40},{56,48},{64,56},{72,6... | collective-permute-start | bytes 393224 | tf_op jit(solution)/shard_map/ppermute | solution.py:21
  121.1 1.9 collective-permute-start.7
  123.0 2.0 fusion.34
  125.0 15.2 %scatter_fusion.2 = f32[16,64,128]{2,1,0:T(8,128)S(1)} fusion(f32[16,64,128]{2,1,0:T(8,128)S(1)} %fusion.34, s32[256]{0:T(256)S(1)} %bitcast.182, f32[256]{0:T(256)S(1)} %get-tuple-element.126), kind=kCustom, calls=%fused_computation.2 | custom fusion | flops 256 | bytes 6144 | tf_op jit(solution)/shard_map/scatter-add | solution.py:59
  140.2 10.6 %multiply_add_fusion = (f32[16,64,128]{2,1,0:T(8,128)S(1)}, f32[16,64,128]{2,1,0:T(8,128)}, f32[16,64,128]{2,1,0:T(8,128)S(1)}) fusion(f32[16,64,128]{2,1,0:T(8,128)S(1)} %copy-done, f32[16,64,128]{2,1,0:T(8,128)S(1)} %scatter-add.44, f32[16,64,128]{2,1,0:T(8,128)} %copy-done.3, f32[4,64,128]{2,1,0:T(8,128)} %collective-permute-done.7, ...), kind=kLoop, calls=%fused_computation.602 | loop fusion | flops 6553600 | bytes 3932160 | tf_op jit(solution)/shard_map/add | solution.py:86
  150.9 6.1 %collective-permute-start.14 = (f32[4,64,128]{2,1,0:T(8,128)S(1)}, f32[4,64,128]{2,1,0:T(8,128)S(1)}, u32[]{:S(2)}, u32[]{:S(2)}) collective-permute-start(f32[4,64,128]{2,1,0:T(8,128)S(1)} %get-tuple-element.53), channel_id=1, source_target_pairs={{8,0},{16,8},{24,16},{32,24},{40,32},{48,40},{56,48},{64,56},{72,6... | collective-permute-start | bytes 393224 | tf_op jit(solution)/shard_map/ppermute | solution.py:21
  156.9 2.1 collective-permute-start.15
  161.7 0.7 fusion.361
  162.4 6.0 %collective-permute-start.8 = (f32[4,64,128]{2,1,0:T(8,128)}, f32[4,64,128]{2,1,0:T(8,128)S(1)}, u32[]{:S(2)}, u32[]{:S(2)}) collective-permute-start(f32[4,64,128]{2,1,0:T(8,128)} %get-tuple-element.62), channel_id=1, source_target_pairs={{8,0},{16,8},{24,16},{32,24},{40,32},{48,40},{56,48},{64,56},{72,6... | collective-permute-start | bytes 393224 | tf_op jit(solution)/shard_map/ppermute | solution.py:21
  168.5 1.9 collective-permute-start.9
  170.4 2.2 fusion.9
  172.7 15.2 %scatter_fusion.3 = f32[16,64,128]{2,1,0:T(8,128)S(1)} fusion(f32[16,64,128]{2,1,0:T(8,128)S(1)} %fusion.9, s32[256]{0:T(256)S(1)} %bitcast.183, f32[256]{0:T(256)S(1)} %get-tuple-element.43), kind=kCustom, calls=%fused_computation.3 | custom fusion | flops 256 | bytes 6144 | tf_op jit(solution)/shard_map/scatter-add | solution.py:59
  187.9 3.9 fusion.87
  191.9 1.1 fusion.357
  193.0 1.2 convolution_bitcast_fusion
  194.2 1.4 convolution_bitcast_fusion.1
  195.6 48.2 %reduce-scatter.2.cloned.1.call-done = f32[16,8,128]{2,1,0:T(8,128)} async-done(((f32[16,64,128]{2,1,0:T(8,128)}), f32[16,8,128]{2,1,0:T(8,128)}) %reduce-scatter.2.cloned.1.call-update) | async-done | bytes 65552 | tf_op jit(solution)/shard_map/reduce_scatter | solution.py:98
  243.7 0.8 broadcast_multiply_fusion
  245.4 73.3 %psum.7 = f32[12,5]{0,1:T(8,128)S(1)} all-reduce(f32[12,5]{0,1:T(8,128)S(1)} %pad_maximum_fusion.16), channel_id=1, replica_groups=mesh['depth'=32,'shot'=8] {'depth','shot'}, use_global_device_ids=true, to_apply=%region_8.9 | all-reduce | flops 60 | bytes 480 | tf_op jit(solution)/shard_map/psum | solution.py:110
  318.8 0.7 fusion.366
  319.5 0.7 fusion.367
  320.2 0.7 fusion.365
  359.7 0.7 multiply_add_fusion.2
  360.4 29.8 %all_gather.3 = f32[16,64,128]{2,1,0:T(8,128)S(1)} all-gather(f32[16,8,128]{2,1,0:T(8,128)S(1)} %get-tuple-element.41), channel_id=1, replica_groups=mesh['depth'=32,'shot'=8] {'shot'}, dimensions={1}, use_global_device_ids=true | all-gather | bytes 589824 | tf_op jit(solution)/shard_map/all_gather | solution.py:144
  390.3 0.8 copy.49
  (70 shorter events, 2.7 us)
Async XLA Ops:
  7.2 236.6 %reduce-scatter.2.cloned.1.call-start = ((), (), s32[]{:S(2)}) async-start(), calls=%async_computation.1 | async-start | bytes 589824 | tf_op jit(solution)/shard_map/reduce_scatter | solution.py:98
  7.2 20.2 %copy-start.10 = (f32[1,16,64,128]{3,2,1,0:T(8,128)S(1)}, f32[1,16,64,128]{3,2,1,0:T(8,128)}, u32[]{:S(2)}) copy-start(f32[1,16,64,128]{3,2,1,0:T(8,128)} %param.19) | copy-start | bytes 1572868
  8.5 6.1 %copy-start.1 = (f32[1,16,64,128]{3,2,1,0:T(8,128)S(1)}, f32[1,16,64,128]{3,2,1,0:T(8,128)}, u32[]{:S(2)}) copy-start(f32[1,16,64,128]{3,2,1,0:T(8,128)} %param.18) | copy-start | bytes 1572868
  8.6 14.1 %copy-start.14 = (f32[1,4,256]{2,1,0:T(4,128)S(1)}, f32[1,4,256]{2,1,0:T(4,128)}, u32[]{:S(2)}) copy-start(f32[1,4,256]{2,1,0:T(4,128)} %param.24) | copy-start | bytes 12292
  8.6 14.1 %copy-start.15 = (s32[1,256]{1,0:T(1,128)S(1)}, s32[1,256]{1,0:T(1,128)}, u32[]{:S(2)}) copy-start(s32[1,256]{1,0:T(1,128)} %param.23) | copy-start | bytes 3076
  8.6 14.7 %copy-start.13 = (f32[1,4]{1,0:T(1,128)S(1)}, f32[1,4]{1,0:T(1,128)}, u32[]{:S(2)}) copy-start(f32[1,4]{1,0:T(1,128)} %param.22) | copy-start | bytes 52
  8.6 18.1 %copy-start.16 = (s32[3]{0:T(128)S(1)}, s32[3]{0:T(128)}, u32[]{:S(2)}) copy-start(s32[3]{0:T(128)} %constant.255.clone.1) | copy-start | bytes 40
  8.6 18.8 %copy-start.2 = (f32[1,16,64,128]{3,2,1,0:T(8,128)S(1)}, f32[1,16,64,128]{3,2,1,0:T(8,128)}, u32[]{:S(2)}) copy-start(f32[1,16,64,128]{3,2,1,0:T(8,128)} %param.20) | copy-start | bytes 1572868
  8.6 18.8 %collective-permute-start = (f32[4,64,128]{2,1,0:T(8,128)S(1)}, f32[4,64,128]{2,1,0:T(8,128)S(1)}, u32[]{:S(2)}, u32[]{:S(2)}) collective-permute-start(f32[4,64,128]{2,1,0:T(8,128)S(1)} %get-tuple-element.70), channel_id=1, source_target_pairs={{8,0},{16,8},{24,16},{32,24},{40,32},{48,40},{56,48},{64,56},{72,6... | collective-permute-start | bytes 393224 | tf_op jit(solution)/shard_map/ppermute | solution.py:21
  12.7 14.7 %collective-permute-start.1 = (f32[4,64,128]{2,1,0:T(8,128)S(1)}, f32[4,64,128]{2,1,0:T(8,128)S(1)}, u32[]{:S(2)}, u32[]{:S(2)}) collective-permute-start(f32[4,64,128]{2,1,0:T(8,128)S(1)} %get-tuple-element.71), channel_id=1, source_target_pairs={{0,8},{8,16},{16,24},{24,32},{32,40},{40,48},{48,56},{56,64},{64,7... | collective-permute-start | bytes 393224 | tf_op jit(solution)/shard_map/ppermute | solution.py:19
  14.7 38.7 %collective-permute-start.2 = (f32[4,64,128]{2,1,0:T(8,128)S(1)}, f32[4,64,128]{2,1,0:T(8,128)S(1)}, u32[]{:S(2)}, u32[]{:S(2)}) collective-permute-start(f32[4,64,128]{2,1,0:T(8,128)S(1)} %get-tuple-element.68), channel_id=1, source_target_pairs={{8,0},{16,8},{24,16},{32,24},{40,32},{48,40},{56,48},{64,56},{72,6... | collective-permute-start | bytes 393224 | tf_op jit(solution)/shard_map/ppermute | solution.py:21
  20.7 32.6 %collective-permute-start.3 = (f32[4,64,128]{2,1,0:T(8,128)S(1)}, f32[4,64,128]{2,1,0:T(8,128)S(1)}, u32[]{:S(2)}, u32[]{:S(2)}) collective-permute-start(f32[4,64,128]{2,1,0:T(8,128)S(1)} %get-tuple-element.69), channel_id=1, source_target_pairs={{0,8},{8,16},{16,24},{24,32},{32,40},{40,48},{48,56},{56,64},{64,7... | collective-permute-start | bytes 393224 | tf_op jit(solution)/shard_map/ppermute | solution.py:19
  29.4 24.0 %copy-start = (f32[16,64,128]{2,1,0:T(8,128)S(1)}, f32[16,64,128]{2,1,0:T(8,128)}, u32[]{:S(2)}) copy-start(f32[16,64,128]{2,1,0:T(8,128)} %param.16) | copy-start | bytes 1572868
  57.0 19.4 %copy-start.6 = (f32[16,64,128]{2,1,0:T(8,128)}, f32[16,64,128]{2,1,0:T(8,128)S(1)}, u32[]{:S(2)}) copy-start(f32[16,64,128]{2,1,0:T(8,128)S(1)} %get-tuple-element.61) | copy-start | bytes 1572868
  59.8 16.6 %collective-permute-start.10 = (f32[4,64,128]{2,1,0:T(8,128)S(1)}, f32[4,64,128]{2,1,0:T(8,128)S(1)}, u32[]{:S(2)}, u32[]{:S(2)}) collective-permute-start(f32[4,64,128]{2,1,0:T(8,128)S(1)} %get-tuple-element.59), channel_id=1, source_target_pairs={{8,0},{16,8},{24,16},{32,24},{40,32},{48,40},{56,48},{64,56},{72,6... | collective-permute-start | bytes 393224 | tf_op jit(solution)/shard_map/ppermute | solution.py:21
  65.9 10.6 %collective-permute-start.11 = (f32[4,64,128]{2,1,0:T(8,128)S(1)}, f32[4,64,128]{2,1,0:T(8,128)S(1)}, u32[]{:S(2)}, u32[]{:S(2)}) collective-permute-start(f32[4,64,128]{2,1,0:T(8,128)S(1)} %get-tuple-element.60), channel_id=1, source_target_pairs={{0,8},{8,16},{16,24},{24,32},{32,40},{40,48},{48,56},{56,64},{64,7... | collective-permute-start | bytes 393224 | tf_op jit(solution)/shard_map/ppermute | solution.py:19
  68.5 32.4 %collective-permute-start.4 = (f32[4,64,128]{2,1,0:T(8,128)}, f32[4,64,128]{2,1,0:T(8,128)S(1)}, u32[]{:S(2)}, u32[]{:S(2)}) collective-permute-start(f32[4,64,128]{2,1,0:T(8,128)} %get-tuple-element.66), channel_id=1, source_target_pairs={{8,0},{16,8},{24,16},{32,24},{40,32},{48,40},{56,48},{64,56},{72,6... | collective-permute-start | bytes 393224 | tf_op jit(solution)/shard_map/ppermute | solution.py:21
  74.5 26.3 %collective-permute-start.5 = (f32[4,64,128]{2,1,0:T(8,128)S(1)}, f32[4,64,128]{2,1,0:T(8,128)S(1)}, u32[]{:S(2)}, u32[]{:S(2)}) collective-permute-start(f32[4,64,128]{2,1,0:T(8,128)S(1)} %get-tuple-element.67), channel_id=1, source_target_pairs={{0,8},{8,16},{16,24},{24,32},{32,40},{40,48},{48,56},{56,64},{64,7... | collective-permute-start | bytes 393224 | tf_op jit(solution)/shard_map/ppermute | solution.py:19
  103.6 9.3 %copy-start.7 = (f32[16,64,128]{2,1,0:T(8,128)}, f32[16,64,128]{2,1,0:T(8,128)S(1)}, u32[]{:S(2)}) copy-start(f32[16,64,128]{2,1,0:T(8,128)S(1)} %get-tuple-element.58) | copy-start | bytes 1572868
  103.6 19.4 %collective-permute-start.12 = (f32[4,64,128]{2,1,0:T(8,128)S(1)}, f32[4,64,128]{2,1,0:T(8,128)S(1)}, u32[]{:S(2)}, u32[]{:S(2)}) collective-permute-start(f32[4,64,128]{2,1,0:T(8,128)S(1)} %get-tuple-element.56), channel_id=1, source_target_pairs={{8,0},{16,8},{24,16},{32,24},{40,32},{48,40},{56,48},{64,56},{72,6... | collective-permute-start | bytes 393224 | tf_op jit(solution)/shard_map/ppermute | solution.py:21
  109.7 13.3 %collective-permute-start.13 = (f32[4,64,128]{2,1,0:T(8,128)S(1)}, f32[4,64,128]{2,1,0:T(8,128)S(1)}, u32[]{:S(2)}, u32[]{:S(2)}) collective-permute-start(f32[4,64,128]{2,1,0:T(8,128)S(1)} %get-tuple-element.57), channel_id=1, source_target_pairs={{0,8},{8,16},{16,24},{24,32},{32,40},{40,48},{48,56},{56,64},{64,7... | collective-permute-start | bytes 393224 | tf_op jit(solution)/shard_map/ppermute | solution.py:19
  114.3 10.7 %copy-start.3 = (f32[16,64,128]{2,1,0:T(8,128)}, f32[16,64,128]{2,1,0:T(8,128)S(1)}, u32[]{:S(2)}) copy-start(f32[16,64,128]{2,1,0:T(8,128)S(1)} %scatter-add.45) | copy-start | bytes 1572868
  114.3 8.7 %copy-start.8 = (f32[16,64,128]{2,1,0:T(8,128)S(1)}, f32[16,64,128]{2,1,0:T(8,128)}, u32[]{:S(2)}) copy-start(f32[16,64,128]{2,1,0:T(8,128)} %copy-done.7) | copy-start | bytes 1572868
  115.0 25.2 %collective-permute-start.6 = (f32[4,64,128]{2,1,0:T(8,128)}, f32[4,64,128]{2,1,0:T(8,128)S(1)}, u32[]{:S(2)}, u32[]{:S(2)}) collective-permute-start(f32[4,64,128]{2,1,0:T(8,128)} %get-tuple-element.64), channel_id=1, source_target_pairs={{8,0},{16,8},{24,16},{32,24},{40,32},{48,40},{56,48},{64,56},{72,6... | collective-permute-start | bytes 393224 | tf_op jit(solution)/shard_map/ppermute | solution.py:21
  121.1 19.2 %collective-permute-start.7 = (f32[4,64,128]{2,1,0:T(8,128)}, f32[4,64,128]{2,1,0:T(8,128)}, u32[]{:S(2)}, u32[]{:S(2)}) collective-permute-start(f32[4,64,128]{2,1,0:T(8,128)} %get-tuple-element.65), channel_id=1, source_target_pairs={{0,8},{8,16},{16,24},{24,32},{32,40},{40,48},{48,56},{56,64},{64,7... | collective-permute-start | bytes 393224 | tf_op jit(solution)/shard_map/ppermute | solution.py:19
  150.8 9.5 %copy-start.4 = (f32[16,64,128]{2,1,0:T(8,128)}, f32[16,64,128]{2,1,0:T(8,128)S(1)}, u32[]{:S(2)}) copy-start(f32[16,64,128]{2,1,0:T(8,128)S(1)} %get-tuple-element.55) | copy-start | bytes 1572868
  150.9 19.6 %collective-permute-start.14 = (f32[4,64,128]{2,1,0:T(8,128)S(1)}, f32[4,64,128]{2,1,0:T(8,128)S(1)}, u32[]{:S(2)}, u32[]{:S(2)}) collective-permute-start(f32[4,64,128]{2,1,0:T(8,128)S(1)} %get-tuple-element.53), channel_id=1, source_target_pairs={{8,0},{16,8},{24,16},{32,24},{40,32},{48,40},{56,48},{64,56},{72,6... | collective-permute-start | bytes 393224 | tf_op jit(solution)/shard_map/ppermute | solution.py:21
  156.9 13.5 %collective-permute-start.15 = (f32[4,64,128]{2,1,0:T(8,128)S(1)}, f32[4,64,128]{2,1,0:T(8,128)}, u32[]{:S(2)}, u32[]{:S(2)}) collective-permute-start(f32[4,64,128]{2,1,0:T(8,128)S(1)} %get-tuple-element.54), channel_id=1, source_target_pairs={{0,8},{8,16},{16,24},{24,32},{32,40},{40,48},{48,56},{56,64},{64,7... | collective-permute-start | bytes 393224 | tf_op jit(solution)/shard_map/ppermute | solution.py:19
  161.7 8.7 %copy-start.5 = (f32[16,64,128]{2,1,0:T(8,128)S(1)}, f32[16,64,128]{2,1,0:T(8,128)}, u32[]{:S(2)}) copy-start(f32[16,64,128]{2,1,0:T(8,128)} %copy-done.4) | copy-start | bytes 1572868
  162.4 25.5 %collective-permute-start.8 = (f32[4,64,128]{2,1,0:T(8,128)}, f32[4,64,128]{2,1,0:T(8,128)S(1)}, u32[]{:S(2)}, u32[]{:S(2)}) collective-permute-start(f32[4,64,128]{2,1,0:T(8,128)} %get-tuple-element.62), channel_id=1, source_target_pairs={{8,0},{16,8},{24,16},{32,24},{40,32},{48,40},{56,48},{64,56},{72,6... | collective-permute-start | bytes 393224 | tf_op jit(solution)/shard_map/ppermute | solution.py:21
  168.5 19.4 %collective-permute-start.9 = (f32[4,64,128]{2,1,0:T(8,128)}, f32[4,64,128]{2,1,0:T(8,128)S(1)}, u32[]{:S(2)}, u32[]{:S(2)}) collective-permute-start(f32[4,64,128]{2,1,0:T(8,128)} %get-tuple-element.63), channel_id=1, source_target_pairs={{0,8},{8,16},{16,24},{24,32},{32,40},{40,48},{48,56},{56,64},{64,7... | collective-permute-start | bytes 393224 | tf_op jit(solution)/shard_map/ppermute | solution.py:19
  244.6 111.4 %copy-start.12 = (f32[16,8,128]{2,1,0:T(8,128)}, f32[16,8,128]{2,1,0:T(8,128)S(1)}, u32[]{:S(2)}) copy-start(f32[16,8,128]{2,1,0:T(8,128)S(1)} %broadcast_multiply_fusion) | copy-start | bytes 196612
  244.6 115.1 %copy-start.9 = (f32[2,5,16,8,128]{4,3,2,1,0:T(8,128)S(1)}, f32[2,5,16,8,128]{4,3,2,1,0:T(8,128)}, u32[]{:S(2)}) copy-start(f32[2,5,16,8,128]{4,3,2,1,0:T(8,128)} %param.25) | copy-start | bytes 1966084
  244.6 115.1 %copy-start.11 = (f32[16,8,128]{2,1,0:T(8,128)S(1)}, f32[16,8,128]{2,1,0:T(8,128)}, u32[]{:S(2)}) copy-start(f32[16,8,128]{2,1,0:T(8,128)} %reduce-scatter.2.cloned.1.call-done) | copy-start | bytes 196612
Sparse Core Ops, SparseCore 0:
  192.0 51.6 reduce-scatter.1
where the time goes:
time: 400 us; the launch traced here: 398 us
  other arithmetic  111 us (28%)
  blocking collectives  103 us (26%)
  starting transfers between devices  61.9 us (15%)
  between operations  61.9 us (15%)
  waiting for transfers between devices  48.2 us (12%)
  local copies, waits for them, and re-layouts  9.48 us (2%)
    psum x1, blocking collectives, per_device(): packed = lax.psum(packed, ('depth', 'shot'))  73.3 us
    scatter-add x4, other arithmetic, inject(): volume.at[row_safe, remainder // volume.shape[2], remainder % volume.shap...  69.6 us
    reduce_scatter x1, waiting for transfers between devices, per_device(): lax.psum_scatter(summed, 'shot', scatter_dimension=1, tiled=True)  48.2 us
    ppermute x8, starting transfers between devices, with_halo(): lax.ppermute(head, axis, [((i + 1) % count, i) for i in range(ends)])  46.4 us
    all_gather x1, blocking collectives, per_device(): courant_next = lax.all_gather(next_piece, 'shot', axis=1, tiled=True)  29.8 us
    add x3, other arithmetic, per_device(): wave_new = 2.0 * wave_now - wave_old + courant * laplacian  17 us
    ppermute x8, starting transfers between devices, with_halo(): lax.ppermute(tail, axis, [(i, (i + 1) % count) for i in range(ends)])  15.5 us
    add x4, other arithmetic, per_device(): adjoint_new = 2.0 * adjoint_now - adjoint_old + laplace_core(extended)  15.3 us
  transfers between devices with their start and end apart: 17, of which 1 were waited for; matrix products, arithmetic and copies ran while one was open for 24% of the time, Pallas kernels for 0%

commit v1 on v0

--- a/solution.py
+++ b/solution.py
@@ -107,7 +107,7 @@
     packed = jnp.concatenate(
         [step_change, change_change, step_grad[None], change_grad[None]], axis=0
     )
-    packed = lax.psum(packed, ("depth", "shot"))
+    packed = jnp.sum(lax.all_gather(packed, ("depth", "shot")), axis=0)
     step_change = packed[:PAIRS]
     change_change = packed[PAIRS : 2 * PAIRS]
     step_grad = packed[2 * PAIRS]

time: 400 us -> 962 us (2.40)
  the two profiles are of different devices: /device:TPU:32 before, /device:TPU:128 now
where the time goes in v1:
time: 962 us; the launch traced here: 960 us
  blocking collectives  655 us (68%)
  other arithmetic  123 us (13%)
  starting transfers between devices  70.2 us (7%)
  between operations  61.7 us (6%)
  waiting for transfers between devices  39 us (4%)
    all_gather x1, blocking collectives, per_device(): packed = jnp.sum(lax.all_gather(packed, ('depth', 'shot')), axis=0)  625 us
    scatter-add x4, other arithmetic, inject(): volume.at[row_safe, remainder // volume.shape[2], remainder % volume.shap...  69.3 us
    ppermute x8, starting transfers between devices, with_halo(): lax.ppermute(head, axis, [((i + 1) % count, i) for i in range(ends)])  54.6 us
    reduce_scatter x1, waiting for transfers between devices, per_device(): lax.psum_scatter(summed, 'shot', scatter_dimension=1, tiled=True)  38.9 us
    all_gather x1, blocking collectives, per_device(): courant_next = lax.all_gather(next_piece, 'shot', axis=1, tiled=True)  29.8 us
    add x4, other arithmetic, per_device(): adjoint_new = 2.0 * adjoint_now - adjoint_old + laplace_core(extended)  28.2 us
  transfers between devices with their start and end apart: 17, of which 1 were waited for; matrix products, arithmetic and copies ran while one was open for 11% of the time, Pallas kernels for 0%

profile of v1, /device:TPU:128, one launch (start us, length us, event | category | flops | bytes accessed | tf_op | source)
XLA Modules:
  0.0 960.5 jit_solution(6491742489121263552)
XLA Ops:
  7.3 1.4 bitcast_multiply_fusion
  8.7 3.9 collective-permute-start
  12.6 1.9 collective-permute-start.1
  14.6 7.3 collective-permute-start.2
  21.8 1.9 collective-permute-start.3
  27.7 0.8 and_reduce_fusion
  28.4 1.9 fusion.184
  30.4 23.9 %scatter_fusion = f32[16,64,128]{2,1,0:T(8,128)S(1)} fusion(f32[16,64,128]{2,1,0:T(8,128)S(1)} %fusion.184, s32[256]{0:T(256)S(1)} %bitcast.182, f32[256]{0:T(256)} %get-tuple-element.128), kind=kCustom, calls=%fused_computation | custom fusion | flops 256 | bytes 6144 | tf_op jit(solution)/shard_map/scatter-add | solution.py:59
  54.3 3.7 fusion.348
  58.0 0.7 dynamic-slice.24
  60.7 7.2 collective-permute-start.10
  68.0 1.9 collective-permute-start.11
  69.9 0.7 fusion.363
  70.6 7.2 collective-permute-start.4
  77.9 1.9 collective-permute-start.5
  79.8 9.0 fusion.59
  88.9 15.1 %scatter_fusion.1 = f32[16,64,128]{2,1,0:T(8,128)S(1)} fusion(f32[16,64,128]{2,1,0:T(8,128)S(1)} %fusion.59, s32[256]{0:T(256)S(1)} %bitcast.183, f32[256]{0:T(256)S(1)} %get-tuple-element.127), kind=kCustom, calls=%fused_computation.1 | custom fusion | flops 256 | bytes 6144 | tf_op jit(solution)/shard_map/scatter-add | solution.py:59
  104.0 2.7 multiply_add_fusion.1
  106.7 7.2 collective-permute-start.12
  114.0 1.9 collective-permute-start.13
  115.9 0.6 dynamic-slice.25
  118.6 0.8 fusion.362
  119.4 7.2 collective-permute-start.6
  126.6 2.1 collective-permute-start.7
  128.8 8.2 fusion.34
  136.9 15.1 %scatter_fusion.2 = f32[16,64,128]{2,1,0:T(8,128)S(1)} fusion(f32[16,64,128]{2,1,0:T(8,128)S(1)} %fusion.34, s32[256]{0:T(256)S(1)} %bitcast.184, f32[256]{0:T(256)S(1)} %get-tuple-element.126), kind=kCustom, calls=%fused_computation.2 | custom fusion | flops 256 | bytes 6144 | tf_op jit(solution)/shard_map/scatter-add | solution.py:59
  152.1 10.1 %multiply_add_fusion = (f32[16,64,128]{2,1,0:T(8,128)S(1)}, f32[16,64,128]{2,1,0:T(8,128)}, f32[16,64,128]{2,1,0:T(8,128)S(1)}) fusion(f32[16,64,128]{2,1,0:T(8,128)S(1)} %copy-done, f32[16,64,128]{2,1,0:T(8,128)S(1)} %scatter-add.44, f32[16,64,128]{2,1,0:T(8,128)} %copy-done.3, f32[4,64,128]{2,1,0:T(8,128)} %collective-permute-done.7, ...), kind=kLoop, calls=%fused_computation.602 | loop fusion | flops 6553600 | bytes 3932160 | tf_op jit(solution)/shard_map/add | solution.py:86
  162.2 7.2 collective-permute-start.14
  169.5 1.9 collective-permute-start.15
  171.4 0.6 dynamic-slice.26
  174.1 0.7 fusion.361
  174.8 7.2 collective-permute-start.8
  182.1 1.9 collective-permute-start.9
  184.0 9.1 fusion.9
  193.1 15.1 %scatter_fusion.3 = f32[16,64,128]{2,1,0:T(8,128)S(1)} fusion(f32[16,64,128]{2,1,0:T(8,128)S(1)} %fusion.9, s32[256]{0:T(256)S(1)} %bitcast.185, f32[256]{0:T(256)S(1)} %get-tuple-element.43), kind=kCustom, calls=%fused_computation.3 | custom fusion | flops 256 | bytes 6144 | tf_op jit(solution)/shard_map/scatter-add | solution.py:59
  208.2 3.9 fusion.87
  212.2 1.1 fusion.357
  213.3 1.2 convolution_bitcast_fusion
  214.5 1.4 convolution_bitcast_fusion.1
  215.9 38.9 %reduce-scatter.2.cloned.1.call-done = f32[16,8,128]{2,1,0:T(8,128)} async-done(((f32[16,64,128]{2,1,0:T(8,128)}), f32[16,8,128]{2,1,0:T(8,128)}) %reduce-scatter.2.cloned.1.call-update) | async-done | bytes 65552 | tf_op jit(solution)/shard_map/reduce_scatter | solution.py:98
  254.8 0.8 broadcast_multiply_fusion
  256.5 624.8 %all-gather.1 = f32[256,12,5]{1,2,0:T(8,128)S(1)} all-gather(f32[1,12,5]{1,2,0:T(8,128)S(1)} %maximum_bitcast_fusion), channel_id=2, replica_groups=mesh['depth'=32,'shot'=8] {'depth','shot'}, dimensions={0}, use_global_device_ids=true | all-gather | bytes 61680 | tf_op jit(solution)/shard_map/all_gather | solution.py:110
  881.6 0.7 fusion.366
  882.3 0.7 fusion.367
  883.0 0.7 fusion.365
  922.4 0.7 multiply_add_fusion.2
  923.1 29.8 %all_gather.11 = f32[16,64,128]{2,1,0:T(8,128)S(1)} all-gather(f32[16,8,128]{2,1,0:T(8,128)S(1)} %get-tuple-element.41), channel_id=1, replica_groups=mesh['depth'=32,'shot'=8] {'shot'}, dimensions={1}, use_global_device_ids=true | all-gather | bytes 589824 | tf_op jit(solution)/shard_map/all_gather | solution.py:144
  952.8 0.8 copy.54
  (67 shorter events, 3.0 us)
Async XLA Ops:
  7.2 20.5 %copy-start.14 = (s32[3]{0:T(128)S(1)}, s32[3]{0:T(128)}, u32[]{:S(2)}) copy-start(s32[3]{0:T(128)} %constant.255.clone.1) | copy-start | bytes 40
  7.2 21.2 %copy-start.2 = (f32[1,16,64,128]{3,2,1,0:T(8,128)S(1)}, f32[1,16,64,128]{3,2,1,0:T(8,128)}, u32[]{:S(2)}) copy-start(f32[1,16,64,128]{3,2,1,0:T(8,128)} %param.20) | copy-start | bytes 1572868
  7.2 7.3 copy-start.1
  7.2 16.6 %copy-start.12 = (f32[1,4,256]{2,1,0:T(4,128)S(1)}, f32[1,4,256]{2,1,0:T(4,128)}, u32[]{:S(2)}) copy-start(f32[1,4,256]{2,1,0:T(4,128)} %param.24) | copy-start | bytes 12292
  7.2 16.6 %copy-start.13 = (s32[1,256]{1,0:T(1,128)S(1)}, s32[1,256]{1,0:T(1,128)}, u32[]{:S(2)}) copy-start(s32[1,256]{1,0:T(1,128)} %param.23) | copy-start | bytes 3076
  7.2 17.2 %copy-start.11 = (f32[1,4]{1,0:T(1,128)S(1)}, f32[1,4]{1,0:T(1,128)}, u32[]{:S(2)}) copy-start(f32[1,4]{1,0:T(1,128)} %param.22) | copy-start | bytes 52
  7.2 21.2 %copy-start.8 = (f32[1,16,64,128]{3,2,1,0:T(8,128)S(1)}, f32[1,16,64,128]{3,2,1,0:T(8,128)}, u32[]{:S(2)}) copy-start(f32[1,16,64,128]{3,2,1,0:T(8,128)} %param.19) | copy-start | bytes 1572868
  7.2 247.6 %reduce-scatter.2.cloned.1.call-start = ((), (), s32[]{:S(2)}) async-start(), calls=%async_computation.1 | async-start | bytes 589824 | tf_op jit(solution)/shard_map/reduce_scatter | solution.py:98
  8.7 19.7 %collective-permute-start = (f32[4,64,128]{2,1,0:T(8,128)S(1)}, f32[4,64,128]{2,1,0:T(8,128)S(1)}, u32[]{:S(2)}, u32[]{:S(2)}) collective-permute-start(f32[4,64,128]{2,1,0:T(8,128)S(1)} %get-tuple-element.70), channel_id=1, source_target_pairs={{8,0},{16,8},{24,16},{32,24},{40,32},{48,40},{56,48},{64,56},{72,6... | collective-permute-start | bytes 393224 | tf_op jit(solution)/shard_map/ppermute | solution.py:21
  12.6 15.8 %collective-permute-start.1 = (f32[4,64,128]{2,1,0:T(8,128)S(1)}, f32[4,64,128]{2,1,0:T(8,128)S(1)}, u32[]{:S(2)}, u32[]{:S(2)}) collective-permute-start(f32[4,64,128]{2,1,0:T(8,128)S(1)} %get-tuple-element.71), channel_id=1, source_target_pairs={{0,8},{8,16},{16,24},{24,32},{32,40},{40,48},{48,56},{56,64},{64,7... | collective-permute-start | bytes 393224 | tf_op jit(solution)/shard_map/ppermute | solution.py:19
  14.6 39.7 %collective-permute-start.2 = (f32[4,64,128]{2,1,0:T(8,128)S(1)}, f32[4,64,128]{2,1,0:T(8,128)S(1)}, u32[]{:S(2)}, u32[]{:S(2)}) collective-permute-start(f32[4,64,128]{2,1,0:T(8,128)S(1)} %get-tuple-element.68), channel_id=1, source_target_pairs={{8,0},{16,8},{24,16},{32,24},{40,32},{48,40},{56,48},{64,56},{72,6... | collective-permute-start | bytes 393224 | tf_op jit(solution)/shard_map/ppermute | solution.py:21
  21.8 32.4 %collective-permute-start.3 = (f32[4,64,128]{2,1,0:T(8,128)S(1)}, f32[4,64,128]{2,1,0:T(8,128)S(1)}, u32[]{:S(2)}, u32[]{:S(2)}) collective-permute-start(f32[4,64,128]{2,1,0:T(8,128)S(1)} %get-tuple-element.69), channel_id=1, source_target_pairs={{0,8},{8,16},{16,24},{24,32},{32,40},{40,48},{48,56},{56,64},{64,7... | collective-permute-start | bytes 393224 | tf_op jit(solution)/shard_map/ppermute | solution.py:19
  30.4 23.9 %copy-start = (f32[16,64,128]{2,1,0:T(8,128)S(1)}, f32[16,64,128]{2,1,0:T(8,128)}, u32[]{:S(2)}) copy-start(f32[16,64,128]{2,1,0:T(8,128)} %param.16) | copy-start | bytes 1572868
  58.0 21.8 %copy-start.5 = (f32[16,64,128]{2,1,0:T(8,128)}, f32[16,64,128]{2,1,0:T(8,128)S(1)}, u32[]{:S(2)}) copy-start(f32[16,64,128]{2,1,0:T(8,128)S(1)} %get-tuple-element.61) | copy-start | bytes 1572868
  60.7 19.0 %collective-permute-start.10 = (f32[4,64,128]{2,1,0:T(8,128)S(1)}, f32[4,64,128]{2,1,0:T(8,128)S(1)}, u32[]{:S(2)}, u32[]{:S(2)}) collective-permute-start(f32[4,64,128]{2,1,0:T(8,128)S(1)} %get-tuple-element.59), channel_id=1, source_target_pairs={{8,0},{16,8},{24,16},{32,24},{40,32},{48,40},{56,48},{64,56},{72,6... | collective-permute-start | bytes 393224 | tf_op jit(solution)/shard_map/ppermute | solution.py:21
  68.0 11.8 %collective-permute-start.11 = (f32[4,64,128]{2,1,0:T(8,128)S(1)}, f32[4,64,128]{2,1,0:T(8,128)S(1)}, u32[]{:S(2)}, u32[]{:S(2)}) collective-permute-start(f32[4,64,128]{2,1,0:T(8,128)S(1)} %get-tuple-element.60), channel_id=1, source_target_pairs={{0,8},{8,16},{16,24},{24,32},{32,40},{40,48},{48,56},{56,64},{64,7... | collective-permute-start | bytes 393224 | tf_op jit(solution)/shard_map/ppermute | solution.py:19
  70.6 33.4 %collective-permute-start.4 = (f32[4,64,128]{2,1,0:T(8,128)}, f32[4,64,128]{2,1,0:T(8,128)S(1)}, u32[]{:S(2)}, u32[]{:S(2)}) collective-permute-start(f32[4,64,128]{2,1,0:T(8,128)} %get-tuple-element.66), channel_id=1, source_target_pairs={{8,0},{16,8},{24,16},{32,24},{40,32},{48,40},{56,48},{64,56},{72,6... | collective-permute-start | bytes 393224 | tf_op jit(solution)/shard_map/ppermute | solution.py:21
  77.9 26.2 %collective-permute-start.5 = (f32[4,64,128]{2,1,0:T(8,128)S(1)}, f32[4,64,128]{2,1,0:T(8,128)S(1)}, u32[]{:S(2)}, u32[]{:S(2)}) collective-permute-start(f32[4,64,128]{2,1,0:T(8,128)S(1)} %get-tuple-element.67), channel_id=1, source_target_pairs={{0,8},{8,16},{16,24},{24,32},{32,40},{40,48},{48,56},{56,64},{64,7... | collective-permute-start | bytes 393224 | tf_op jit(solution)/shard_map/ppermute | solution.py:19
  106.7 10.5 %copy-start.6 = (f32[16,64,128]{2,1,0:T(8,128)}, f32[16,64,128]{2,1,0:T(8,128)S(1)}, u32[]{:S(2)}) copy-start(f32[16,64,128]{2,1,0:T(8,128)S(1)} %get-tuple-element.58) | copy-start | bytes 1572868
  106.7 22.0 %collective-permute-start.12 = (f32[4,64,128]{2,1,0:T(8,128)S(1)}, f32[4,64,128]{2,1,0:T(8,128)S(1)}, u32[]{:S(2)}, u32[]{:S(2)}) collective-permute-start(f32[4,64,128]{2,1,0:T(8,128)S(1)} %get-tuple-element.56), channel_id=1, source_target_pairs={{8,0},{16,8},{24,16},{32,24},{40,32},{48,40},{56,48},{64,56},{72,6... | collective-permute-start | bytes 393224 | tf_op jit(solution)/shard_map/ppermute | solution.py:21
  114.0 14.8 %collective-permute-start.13 = (f32[4,64,128]{2,1,0:T(8,128)S(1)}, f32[4,64,128]{2,1,0:T(8,128)S(1)}, u32[]{:S(2)}, u32[]{:S(2)}) collective-permute-start(f32[4,64,128]{2,1,0:T(8,128)S(1)} %get-tuple-element.57), channel_id=1, source_target_pairs={{0,8},{8,16},{16,24},{24,32},{32,40},{40,48},{48,56},{56,64},{64,7... | collective-permute-start | bytes 393224 | tf_op jit(solution)/shard_map/ppermute | solution.py:19
  118.6 18.3 %copy-start.3 = (f32[16,64,128]{2,1,0:T(8,128)}, f32[16,64,128]{2,1,0:T(8,128)S(1)}, u32[]{:S(2)}) copy-start(f32[16,64,128]{2,1,0:T(8,128)S(1)} %scatter-add.45) | copy-start | bytes 1572868
  119.4 32.7 %collective-permute-start.6 = (f32[4,64,128]{2,1,0:T(8,128)}, f32[4,64,128]{2,1,0:T(8,128)S(1)}, u32[]{:S(2)}, u32[]{:S(2)}) collective-permute-start(f32[4,64,128]{2,1,0:T(8,128)} %get-tuple-element.64), channel_id=1, source_target_pairs={{8,0},{16,8},{24,16},{32,24},{40,32},{48,40},{56,48},{64,56},{72,6... | collective-permute-start | bytes 393224 | tf_op jit(solution)/shard_map/ppermute | solution.py:21
  126.6 25.5 %collective-permute-start.7 = (f32[4,64,128]{2,1,0:T(8,128)}, f32[4,64,128]{2,1,0:T(8,128)}, u32[]{:S(2)}, u32[]{:S(2)}) collective-permute-start(f32[4,64,128]{2,1,0:T(8,128)} %get-tuple-element.65), channel_id=1, source_target_pairs={{0,8},{8,16},{16,24},{24,32},{32,40},{40,48},{48,56},{56,64},{64,7... | collective-permute-start | bytes 393224 | tf_op jit(solution)/shard_map/ppermute | solution.py:19
  162.2 10.5 %copy-start.4 = (f32[16,64,128]{2,1,0:T(8,128)}, f32[16,64,128]{2,1,0:T(8,128)S(1)}, u32[]{:S(2)}) copy-start(f32[16,64,128]{2,1,0:T(8,128)S(1)} %get-tuple-element.55) | copy-start | bytes 1572868
  162.2 21.8 %collective-permute-start.14 = (f32[4,64,128]{2,1,0:T(8,128)S(1)}, f32[4,64,128]{2,1,0:T(8,128)S(1)}, u32[]{:S(2)}, u32[]{:S(2)}) collective-permute-start(f32[4,64,128]{2,1,0:T(8,128)S(1)} %get-tuple-element.53), channel_id=1, source_target_pairs={{8,0},{16,8},{24,16},{32,24},{40,32},{48,40},{56,48},{64,56},{72,6... | collective-permute-start | bytes 393224 | tf_op jit(solution)/shard_map/ppermute | solution.py:21
  169.5 14.5 %collective-permute-start.15 = (f32[4,64,128]{2,1,0:T(8,128)S(1)}, f32[4,64,128]{2,1,0:T(8,128)}, u32[]{:S(2)}, u32[]{:S(2)}) collective-permute-start(f32[4,64,128]{2,1,0:T(8,128)S(1)} %get-tuple-element.54), channel_id=1, source_target_pairs={{0,8},{8,16},{16,24},{24,32},{32,40},{40,48},{48,56},{56,64},{64,7... | collective-permute-start | bytes 393224 | tf_op jit(solution)/shard_map/ppermute | solution.py:19
  174.8 33.4 %collective-permute-start.8 = (f32[4,64,128]{2,1,0:T(8,128)}, f32[4,64,128]{2,1,0:T(8,128)S(1)}, u32[]{:S(2)}, u32[]{:S(2)}) collective-permute-start(f32[4,64,128]{2,1,0:T(8,128)} %get-tuple-element.62), channel_id=1, source_target_pairs={{8,0},{16,8},{24,16},{32,24},{40,32},{48,40},{56,48},{64,56},{72,6... | collective-permute-start | bytes 393224 | tf_op jit(solution)/shard_map/ppermute | solution.py:21
  182.1 26.2 %collective-permute-start.9 = (f32[4,64,128]{2,1,0:T(8,128)}, f32[4,64,128]{2,1,0:T(8,128)S(1)}, u32[]{:S(2)}, u32[]{:S(2)}) collective-permute-start(f32[4,64,128]{2,1,0:T(8,128)} %get-tuple-element.63), channel_id=1, source_target_pairs={{0,8},{8,16},{16,24},{24,32},{32,40},{40,48},{48,56},{56,64},{64,7... | collective-permute-start | bytes 393224 | tf_op jit(solution)/shard_map/ppermute | solution.py:19
  255.7 625.9 %copy-start.10 = (f32[16,8,128]{2,1,0:T(8,128)}, f32[16,8,128]{2,1,0:T(8,128)S(1)}, u32[]{:S(2)}) copy-start(f32[16,8,128]{2,1,0:T(8,128)S(1)} %broadcast_multiply_fusion) | copy-start | bytes 196612
  256.5 665.9 %copy-start.7 = (f32[2,5,16,8,128]{4,3,2,1,0:T(8,128)S(1)}, f32[2,5,16,8,128]{4,3,2,1,0:T(8,128)}, u32[]{:S(2)}) copy-start(f32[2,5,16,8,128]{4,3,2,1,0:T(8,128)} %param.25) | copy-start | bytes 1966084
  256.5 665.9 %copy-start.9 = (f32[16,8,128]{2,1,0:T(8,128)S(1)}, f32[16,8,128]{2,1,0:T(8,128)}, u32[]{:S(2)}) copy-start(f32[16,8,128]{2,1,0:T(8,128)} %reduce-scatter.2.cloned.1.call-done) | copy-start | bytes 196612
Sparse Core Ops, SparseCore 0:
  212.3 42.4 reduce-scatter.1
